TPU v7x, 32 devices: a whole 2x2x4 slice. The times are simulated.
32 devices in a mesh: dp: 4 (over x, core), tensor: 8 (over z, y).
Axes of the slice: x: 2, y: 2, z: 4, core: 2. Of those that a mesh axis runs over, the one named last changes fastest.
Arguments:
- block_input: bfloat16 [6144, 2048], P(('dp', 'tensor')), may hold values from -6 to 6
- norm_gain: bfloat16 [2048], P('dp'), may hold values from 0.5 to 1.5
- in_weight: bfloat16 [2, 2048, 4096], P(None, 'dp', 'tensor'), may hold values from -0.125 to 0.125
- conv_weight: bfloat16 [4, 32, 128], P(None, 'tensor', 'dp'), may hold values from -0.5 to 0.5
- conv_bias: bfloat16 [32, 128], P('tensor', 'dp'), may hold values from -0.5 to 0.5
- select_weight: bfloat16 [32, 128, 160], P('tensor', 'dp'), may hold values from -0.09375 to 0.09375
- delta_weight: bfloat16 [128, 4096], P('dp', 'tensor'), may hold values from -0.5 to 0.5
- delta_bias: bfloat16 [32, 128], P('tensor', 'dp'), may hold values from -6 to -1
- decay_log: bfloat16 [4096, 16], P('tensor', 'dp'), may hold values from 0 to 2.765625
- skip_weight: bfloat16 [32, 128], P('tensor', 'dp'), may hold values from 0.5 to 1.5
- out_weight: bfloat16 [4096, 2048], P('tensor', 'dp'), may hold values from -0.1875 to 0.1875
- out_cotangent: bfloat16 [6144, 2048], P(('dp', 'tensor')), may hold values from -6 to 6
- seq_lengths: int32 [4, 4], P('dp'), may hold values from 1 to 1152, 1536 in all within a row
- deal_order: int32 [6144], P(('dp', 'tensor')), may hold values from 0 to 6143, as said below
Outputs:
- block_output: bfloat16 [6144, 2048], P(('dp', 'tensor'))
- input_grad: bfloat16 [6144, 2048], P(('dp', 'tensor'))
- norm_gain_grad: float32 [2048], P('dp')
- in_weight_grad: float32 [2, 2048, 4096], P(None, 'dp', 'tensor')
- conv_weight_grad: float32 [4, 32, 128], P(None, 'tensor', 'dp')
- conv_bias_grad: float32 [32, 128], P('tensor', 'dp')
- select_weight_grad: float32 [32, 128, 160], P('tensor', 'dp')
- delta_weight_grad: float32 [128, 4096], P('dp', 'tensor')
- delta_bias_grad: float32 [32, 128], P('tensor', 'dp')
- decay_log_grad: float32 [4096, 16], P('tensor', 'dp')
- skip_weight_grad: float32 [32, 128], P('tensor', 'dp')
- out_weight_grad: float32 [4096, 2048], P('tensor', 'dp')
Inputs may be any that keep to these rules, and one draw needn't show every extreme that they name: A permutation of the tokens: dealt place p holds the token of given place deal_order[p]. p and deal_order[p] lie in the same one of the 8 runs of 192 places inside their blocks of 1536 places, and each aligned run of 192 given places sends exactly 48 tokens to each block of 1536 dealt places. `seq_lengths`: each row sums to 1536; its largest entry is exactly 1152.
All inputs are finite; a program needn't handle non-finite values.
Results may differ from a plain program's by a relative error of at most 0.012.
Values may be sent and summed in bfloat16 or wider, within the bound.
No kernel may reach another device: no remote copies, remote signals or barrier semaphores. Data moves between devices by JAX's collectives and lax.ppermute only.
A program may use at most 320 MiB of HBM per device.

v0:
```python
import jax
import jax.numpy as jnp
from jax import lax
from jax.sharding import PartitionSpec as P

EPSILON = 1e-05
step_span = 16


def to_steps(values):
    blocks = values.shape[0] // step_span
    return jnp.swapaxes(values.reshape((blocks, step_span) + values.shape[1:]), 0, 1)


def from_steps(values):
    swapped = jnp.swapaxes(values, 0, 1)
    return swapped.reshape((-1,) + swapped.shape[2:])


def shifted(values, amount):
    head = jnp.zeros((amount,) + values.shape[1:], values.dtype)
    return jnp.concatenate([head, values[: values.shape[0] - amount]], axis=0)


def unshifted(values, amount):
    tail = jnp.zeros((amount,) + values.shape[1:], values.dtype)
    return jnp.concatenate([values[amount:], tail], axis=0)


def step_terms(delta_step, act_step, b_step, keep_step, decay_rate):
    decays = jnp.exp(delta_step[:, :, None] * decay_rate[None]) * keep_step[:, None, None]
    source = (delta_step * act_step)[:, :, None] * b_step[:, None, :]
    return (decays, source)


def block_starts(totals, finals):

    def combine(earlier, latter):
        return (earlier[0] * latter[0], latter[0] * earlier[1] + latter[1])

    inclusive = lax.associative_scan(combine, (totals, finals))[1]
    return jnp.concatenate([jnp.zeros_like(inclusive[:1]), inclusive[:-1]], axis=0)


def scan_forward(step_size, act_values, b_values, c_values, continues, decay_rate, skip_values):
    step_inputs = (
        to_steps(step_size),
        to_steps(act_values),
        to_steps(b_values),
        to_steps(continues),
    )
    blocks = step_size.shape[0] // step_span
    empty_state = jnp.zeros((blocks,) + decay_rate.shape, jnp.float32)

    def local_step(carried, inputs):
        current, running = carried
        decays, source = step_terms(inputs[0], inputs[1], inputs[2], inputs[3], decay_rate)
        return ((decays * current + source, decays * running), None)

    (finals, totals), unused = lax.scan(
        local_step, (empty_state, jnp.ones_like(empty_state)), step_inputs
    )
    starts = block_starts(totals, finals)

    def output_step(current, inputs):
        delta_step, act_step, b_step, keep_step, c_step = inputs
        decays, source = step_terms(delta_step, act_step, b_step, keep_step, decay_rate)
        current = decays * current + source
        return (
            current,
            jnp.sum(current * c_step[:, None, :], axis=2) + skip_values[None, :] * act_step,
        )

    unused_state, outputs = lax.scan(output_step, starts, step_inputs + (to_steps(c_values),))
    return (from_steps(outputs), starts)


def scan_backward(step_size, act_values, b_values, c_values, continues, decay_rate, starts, grad_y):
    base_inputs = (
        to_steps(step_size),
        to_steps(act_values),
        to_steps(b_values),
        to_steps(continues),
    )
    back_inputs = base_inputs + (to_steps(c_values), to_steps(grad_y))
    empty_state = jnp.zeros(starts.shape, jnp.float32)

    def local_back(carried, inputs):
        incoming, running = carried
        delta_step, act_step, b_step, keep_step, c_step, grad_step = inputs
        decays, source = step_terms(delta_step, act_step, b_step, keep_step, decay_rate)
        adjoint = c_step[:, None, :] * grad_step[:, :, None] + incoming
        return ((decays * adjoint, decays * running), None)

    (outgoing, totals), unused = lax.scan(
        local_back, (empty_state, jnp.ones_like(empty_state)), back_inputs, reverse=True
    )
    arriving = block_starts(totals[::-1], outgoing[::-1])[::-1]

    def state_step(current, inputs):
        decays, source = step_terms(inputs[0], inputs[1], inputs[2], inputs[3], decay_rate)
        return (decays * current + source, current)

    unused_state, previous = lax.scan(state_step, starts, base_inputs)

    def gradient_step(carried, inputs):
        incoming, rate_grad = carried
        delta_step, act_step, b_step, keep_step, c_step, grad_step, prior = inputs
        decays, source = step_terms(delta_step, act_step, b_step, keep_step, decay_rate)
        current = decays * prior + source
        adjoint = c_step[:, None, :] * grad_step[:, :, None] + incoming
        grad_drive = jnp.sum(adjoint * b_step[:, None, :], axis=2)
        grad_b = jnp.sum(adjoint * (delta_step * act_step)[:, :, None], axis=1)
        grad_c = jnp.sum(current * grad_step[:, :, None], axis=1)
        through = adjoint * prior * decays
        grad_decay = jnp.sum(through * decay_rate[None], axis=2)
        rate_grad = rate_grad + jnp.sum(through * delta_step[:, :, None], axis=0)
        return ((decays * adjoint, rate_grad), (grad_drive, grad_b, grad_c, grad_decay))

    rate_start = jnp.zeros(decay_rate.shape, jnp.float32)
    (unused_carry, rate_grad), stacked = lax.scan(
        gradient_step, (arriving, rate_start), back_inputs + (previous,), reverse=True
    )
    grad_drive, grad_b, grad_c, grad_decay = (from_steps(stacked_item) for stacked_item in stacked)
    return (grad_drive, grad_b, grad_c, grad_decay, rate_grad)


def shards(
    block_input,
    norm_gain,
    in_weight,
    conv_weight,
    conv_bias,
    select_weight,
    delta_weight,
    delta_bias,
    decay_log,
    skip_weight,
    out_weight,
    out_cotangent,
    seq_lengths,
    deal_order,
):
    rows_dev = block_input.shape[0]
    dp_size = lax.axis_size("dp")
    tensor_size = lax.axis_size("tensor")
    per_pair = rows_dev // dp_size
    group_tokens = rows_dev * tensor_size
    source_dp = deal_order // group_tokens
    local_row = deal_order % rows_dev
    arrangement = jnp.argsort(source_dp, stable=True)
    restore = jnp.argsort(arrangement)
    requests = local_row[arrangement].reshape(dp_size, per_pair)
    wanted = lax.all_to_all(requests, "dp", split_axis=0, concat_axis=0, tiled=True).reshape(
        rows_dev
    )
    send_rows = block_input[wanted].reshape(dp_size, per_pair, -1)
    send_cot = out_cotangent[wanted].reshape(dp_size, per_pair, -1)
    recv_rows, recv_cot = (
        lax.all_to_all(send_rows, "dp", split_axis=0, concat_axis=0, tiled=True),
        lax.all_to_all(send_cot, "dp", split_axis=0, concat_axis=0, tiled=True),
    )
    dealt_x = recv_rows.reshape(rows_dev, -1)[restore]
    dealt_cot = recv_cot.reshape(rows_dev, -1)[restore]
    (
        gain_full,
        in_full,
        conv_full,
        conv_shift_full,
        select_full,
        delta_full,
        delta_shift_full,
        decay_full,
        skip_full,
        out_full,
    ) = (
        lax.all_gather(norm_gain, "dp", axis=0, tiled=True),
        lax.all_gather(in_weight, "dp", axis=1, tiled=True),
        lax.all_gather(conv_weight, "dp", axis=2, tiled=True),
        lax.all_gather(conv_bias, "dp", axis=1, tiled=True),
        lax.all_gather(select_weight, "dp", axis=1, tiled=True),
        lax.all_gather(delta_weight, "dp", axis=0, tiled=True),
        lax.all_gather(delta_bias, "dp", axis=1, tiled=True),
        lax.all_gather(decay_log, "dp", axis=1, tiled=True),
        lax.all_gather(skip_weight, "dp", axis=1, tiled=True),
        lax.all_gather(out_weight, "dp", axis=1, tiled=True),
    )
    channels = in_full.shape[2]
    kernel_taps = conv_full.shape[0]
    lane_width = conv_shift_full.shape[1]
    select_matrix = select_full.reshape(channels, -1)
    conv_taps = conv_full.astype(jnp.float32).reshape(kernel_taps, channels)
    conv_shift = conv_shift_full.astype(jnp.float32).reshape(channels)
    delta_shift = delta_shift_full.astype(jnp.float32).reshape(channels)
    skip_values = skip_full.astype(jnp.float32).reshape(channels)
    decay_rate = -jnp.exp(decay_full.astype(jnp.float32))
    gain_values = gain_full.astype(jnp.float32)
    rows_float = dealt_x.astype(jnp.float32)
    inverse_rms = lax.rsqrt(jnp.mean(rows_float * rows_float, axis=1, keepdims=True) + EPSILON)
    unit_rows = rows_float * inverse_rms
    normed = (unit_rows * gain_values[None, :]).astype(jnp.bfloat16)
    group_normed = lax.all_gather(normed, "tensor", axis=0, tiled=True)
    lengths_row = seq_lengths[0]
    seq_ends = jnp.cumsum(lengths_row)
    begins = seq_ends - lengths_row
    positions = jnp.arange(group_tokens, dtype=jnp.int32)
    inside = (positions[:, None] >= begins[None, :]) & (positions[:, None] < seq_ends[None, :])
    offset = positions - jnp.sum(jnp.where(inside, begins[None, :], 0), axis=1)
    continues = (offset > 0).astype(jnp.float32)
    projected = jnp.einsum(
        "gd,kdc->gkc", group_normed, in_full, preferred_element_type=jnp.float32
    ).astype(jnp.bfloat16)
    inner_in = projected[:, 0].astype(jnp.float32)
    gate_in = projected[:, 1].astype(jnp.float32)
    masks = [(offset >= tap_index).astype(jnp.float32)[:, None] for tap_index in range(kernel_taps)]
    convolved = conv_shift[None, :]
    for tap_index in range(kernel_taps):
        convolved = (
            convolved
            + conv_taps[tap_index][None, :] * shifted(inner_in, tap_index) * masks[tap_index]
        )
    activated = jax.nn.silu(convolved).astype(jnp.bfloat16)
    act_values = activated.astype(jnp.float32)
    proj_sums = lax.psum(
        jnp.dot(activated, select_matrix, preferred_element_type=jnp.float32), "tensor"
    )
    low_rank = delta_full.shape[0]
    state_size = decay_full.shape[1]
    delta_low = proj_sums[:, :low_rank].astype(jnp.bfloat16)
    b_values = proj_sums[:, low_rank : low_rank + state_size]
    c_values = proj_sums[:, low_rank + state_size :]
    pre_delta = (
        jnp.dot(delta_low, delta_full, preferred_element_type=jnp.float32) + delta_shift[None, :]
    )
    step_size = jax.nn.softplus(pre_delta)
    y_values, starts = scan_forward(
        step_size, act_values, b_values, c_values, continues, decay_rate, skip_values
    )
    gated = (y_values * jax.nn.silu(gate_in)).astype(jnp.bfloat16)
    piece = gated
    mixed = lax.psum_scatter(
        jnp.dot(piece, out_full, preferred_element_type=jnp.float32),
        "tensor",
        scatter_dimension=0,
        tiled=True,
    )
    block_output = (rows_float + mixed).astype(jnp.bfloat16)
    group_normed, group_cot = (
        lax.all_gather(normed, "tensor", axis=0, tiled=True),
        lax.all_gather(dealt_cot, "tensor", axis=0, tiled=True),
    )
    contract_rows = (((0,), (0,)), ((), ()))
    contract_cols = (((1,), (1,)), ((), ()))
    out_weight_grad = lax.dot_general(
        gated, group_cot, contract_rows, preferred_element_type=jnp.float32
    )
    grad_gated = lax.dot_general(
        group_cot, out_full, contract_cols, preferred_element_type=jnp.float32
    )
    gate_sig = jax.nn.sigmoid(gate_in)
    grad_y = grad_gated * gate_in * gate_sig
    grad_gate = grad_gated * y_values * gate_sig * (1.0 + gate_in * (1.0 - gate_sig))
    grad_drive, grad_b, grad_c, grad_decay, rate_grad = scan_backward(
        step_size, act_values, b_values, c_values, continues, decay_rate, starts, grad_y
    )
    decay_log_grad = rate_grad * decay_rate
    skip_grad = jnp.sum(grad_y * act_values, axis=0)
    grad_delta = grad_drive * act_values + grad_decay
    grad_pre = (grad_delta * jax.nn.sigmoid(pre_delta)).astype(jnp.bfloat16)
    delta_bias_grad = jnp.sum(grad_pre.astype(jnp.float32), axis=0)
    delta_weight_grad = lax.dot_general(
        delta_low, grad_pre, contract_rows, preferred_element_type=jnp.float32
    )
    grad_low = lax.dot_general(
        grad_pre, delta_full, contract_cols, preferred_element_type=jnp.float32
    )
    grad_proj = lax.psum(jnp.concatenate([grad_low, grad_b, grad_c], axis=1), "tensor").astype(
        jnp.bfloat16
    )
    select_weight_grad = lax.dot_general(
        activated, grad_proj, contract_rows, preferred_element_type=jnp.float32
    )
    grad_act = grad_drive * step_size + grad_y * skip_values[None, :]
    grad_act = grad_act + lax.dot_general(
        grad_proj, select_matrix, contract_cols, preferred_element_type=jnp.float32
    )
    conv_sig = jax.nn.sigmoid(convolved)
    grad_conv = grad_act * conv_sig * (1.0 + convolved * (1.0 - conv_sig))
    conv_bias_grad = jnp.sum(grad_conv, axis=0)
    tap_grads = []
    grad_inner = jnp.zeros_like(grad_conv)
    for tap_index in range(kernel_taps):
        masked = grad_conv * masks[tap_index]
        tap_grads.append(jnp.sum(masked * shifted(inner_in, tap_index), axis=0))
        grad_inner = grad_inner + unshifted(masked * conv_taps[tap_index][None, :], tap_index)
    conv_weight_grad = jnp.stack(tap_grads, axis=0)
    grad_projected = jnp.stack([grad_inner, grad_gate], axis=1).astype(jnp.bfloat16)
    in_weight_grad = jnp.einsum(
        "gd,gkc->kdc", group_normed, grad_projected, preferred_element_type=jnp.float32
    )
    piece = grad_projected
    grad_normed = lax.psum_scatter(
        jnp.einsum("gkc,kdc->gd", piece, in_full, preferred_element_type=jnp.float32),
        "tensor",
        scatter_dimension=0,
        tiled=True,
    )
    gain_part = jnp.sum(grad_normed * unit_rows, axis=0)
    scaled = grad_normed * gain_values[None, :]
    grad_rows = dealt_cot.astype(jnp.float32) + inverse_rms * (
        scaled - unit_rows * jnp.mean(scaled * unit_rows, axis=1, keepdims=True)
    )
    input_grad = grad_rows.astype(jnp.bfloat16)
    reduced = (
        lax.psum_scatter(gain_part, "dp", scatter_dimension=0, tiled=True),
        lax.psum_scatter(in_weight_grad, "dp", scatter_dimension=1, tiled=True),
        lax.psum_scatter(
            conv_weight_grad.reshape(kernel_taps, -1, lane_width),
            "dp",
            scatter_dimension=2,
            tiled=True,
        ),
        lax.psum_scatter(
            conv_bias_grad.reshape(-1, lane_width), "dp", scatter_dimension=1, tiled=True
        ),
        lax.psum_scatter(
            select_weight_grad.reshape(-1, lane_width, select_weight_grad.shape[1]),
            "dp",
            scatter_dimension=1,
            tiled=True,
        ),
        lax.psum_scatter(delta_weight_grad, "dp", scatter_dimension=0, tiled=True),
        lax.psum_scatter(
            delta_bias_grad.reshape(-1, lane_width), "dp", scatter_dimension=1, tiled=True
        ),
        lax.psum_scatter(decay_log_grad, "dp", scatter_dimension=1, tiled=True),
        lax.psum_scatter(skip_grad.reshape(-1, lane_width), "dp", scatter_dimension=1, tiled=True),
        lax.psum_scatter(out_weight_grad, "dp", scatter_dimension=1, tiled=True),
    )
    gain_grad = lax.psum(reduced[0], "tensor")
    back_out = block_output[arrangement].reshape(dp_size, per_pair, -1)
    back_grad = input_grad[arrangement].reshape(dp_size, per_pair, -1)
    home_out, home_grad = (
        lax.all_to_all(back_out, "dp", split_axis=0, concat_axis=0, tiled=True),
        lax.all_to_all(back_grad, "dp", split_axis=0, concat_axis=0, tiled=True),
    )
    homing = jnp.argsort(wanted)
    final_out = home_out.reshape(rows_dev, -1)[homing]
    final_grad = home_grad.reshape(rows_dev, -1)[homing]
    return (
        final_out,
        final_grad,
        gain_grad,
        reduced[1],
        reduced[2],
        reduced[3],
        reduced[4],
        reduced[5],
        reduced[6],
        reduced[7],
        reduced[8],
        reduced[9],
    )


def solution(mesh):
    return jax.shard_map(
        shards,
        mesh=mesh,
        in_specs=(
            P(("dp", "tensor"), None),
            P("dp"),
            P(None, "dp", "tensor"),
            P(None, "tensor", "dp"),
            P("tensor", "dp"),
            P("tensor", "dp", None),
            P("dp", "tensor"),
            P("tensor", "dp"),
            P("tensor", "dp"),
            P("tensor", "dp"),
            P("tensor", "dp"),
            P(("dp", "tensor"), None),
            P("dp", None),
            P(("dp", "tensor")),
        ),
        out_specs=(
            P(("dp", "tensor"), None),
            P(("dp", "tensor"), None),
            P("dp"),
            P(None, "dp", "tensor"),
            P(None, "tensor", "dp"),
            P("tensor", "dp"),
            P("tensor", "dp", None),
            P("dp", "tensor"),
            P("tensor", "dp"),
            P("tensor", "dp"),
            P("tensor", "dp"),
            P("tensor", "dp"),
        ),
        check_vma=False,
    )
```

profile of v0, /device:TPU:0, one launch (start us, length us, event | category | flops | bytes accessed | tf_op | source)
XLA Modules:
  0.0 2057.3 jit_solution(17485886512966936121)
XLA Ops:
  31.3 18.1 all-gather.2
  54.6 14.1 all_to_all.30
  88.8 68.3 %all-gather.11.cloned.1.call-done = bf16[1536,2048]{1,0:T(8,128)(2,1)} async-done(((bf16[192,2048]{1,0:T(8,128)(2,1)}), bf16[1536,2048]{1,0:T(8,128)(2,1)}) %all-gather.11.cloned.1.call-update) | async-done | bytes 6291472 | tf_op jit(solution)/shard_map/all_gather | solution.py:202
  179.5 101.7 %all-gather.17.cloned.1.call-done = bf16[1536,2048]{1,0:T(8,128)(2,1)} async-done(((bf16[192,2048]{1,0:T(8,128)(2,1)}), bf16[1536,2048]{1,0:T(8,128)(2,1)}) %all-gather.17.cloned.1.call-update) | async-done | bytes 6291472 | tf_op jit(solution)/shard_map/all_gather | solution.py:250
  281.2 13.6 multiply_reduce_fusion.5
  323.0 49.9 %all-reduce.38.cloned.1.call-done = f32[1536,160]{0,1:T(8,128)} async-done(((f32[1536,160]{0,1:T(8,128)}), f32[1536,160]{0,1:T(8,128)}) %all-reduce.38.cloned.1.call-update) | async-done | bytes 983056 | tf_op jit(solution)/shard_map/psum | solution.py:224
  389.5 120.8 %while.81 = (s32[]{:T(128)}, f32[96,512,16]{1,2,0:T(8,128)S(1)}, f32[96,512,16]{1,2,0:T(8,128)}, f32[16,96,512]{2,1,0:T(8,128)}, f32[512,16]{0,1:T(8,128)S(1)}, ...) while((s32[]{:T(128)}, f32[96,512,16]{1,2,0:T(8,128)S(1)}, ...), condition=%wide.region_7.8_spmd.clone, body=%wide.region_6.7_spmd.clone.sunk | while | flops 6340611 | bytes 14011647 | solution.py:60
  593.4 18.5 pad.209
  614.7 24.3 %pad.148 = f32[95,512,16]{1,2,0:T(8,128)} pad(f32[48,512,16]{1,2,0:T(8,128)} %pad_maximum_fusion.3, f32[]{:T(128)} %constant.182.clone.1), padding=0_0_1x0_0_0x0_0_0 | pad | bytes 4685828 | tf_op jit(solution)/shard_map/slice | solution.py:42
  644.8 99.7 %while.82 = (s32[]{:T(128)}, f32[96,512,16]{1,2,0:T(8,128)}, f32[96,512,16]{1,2,0:T(8,128)}, f32[16,96,512]{2,1,0:T(8,128)}, f32[512,16]{0,1:T(8,128)S(1)}, /*in...) while((s32[]{:T(128)}, f32[96,512,16]{1,2,0:T(8,128)}, ...), condition=%wide.region_14.15_spmd.clone, body=%wide.region_13.14_spmd.clone.sunk | while | flops 6291460 | bytes 13815055 | solution.py:95
  801.8 99.8 %while.79 = (s32[]{:T(128)}, f32[96,512,16]{1,2,0:T(8,128)S(1)}, f32[16,96,512]{2,1,0:T(8,128)}, f32[16,96,512]{2,1,0:T(8,128)}, f32[512,16]{0,1:T(8,128)S(1)}, ...) while((s32[]{:T(128)}, f32[96,512,16]{1,2,0:T(8,128)S(1)}, ...), condition=%wide.region_10.11_spmd, body=%wide.region_8.10_spmd.sunk | while | flops 5603330 | bytes 8527613 | solution.py:74
  907.2 101.5 %while.80 = (s32[]{:T(128)}, f32[96,512,16]{1,2,0:T(8,128)S(1)}, f32[16,96,512,16]{2,3,1,0:T(8,128)}, f32[16,96,512]{2,1,0:T(8,128)}, f32[512,16]{0,1:T(8,128)S(...) while((s32[]{:T(128)}, f32[96,512,16]{1,2,0:T(8,128)S(1)}, ...), condition=%wide.region_16.17_spmd, body=%wide.region_15.16_spmd.sunk | while | flops 3981314 | bytes 14012141 | solution.py:104
  1021.0 24.4 %pad.210 = f32[96,512,16]{1,2,0:T(8,128)} pad(f32[48,512,16]{1,2,0:T(8,128)} %add.471, f32[]{:T(128)} %constant.182.clone.1), padding=1_0_1x0_0_0x0_0_0 | pad | bytes 4718596
  1049.3 24.2 %pad.150 = f32[95,512,16]{1,2,0:T(8,128)} pad(f32[48,512,16]{1,2,0:T(8,128)} %pad_maximum_fusion.4, f32[]{:T(128)} %constant.182.clone.1), padding=0_0_1x0_0_0x0_0_0 | pad | bytes 4685828 | tf_op jit(solution)/shard_map/slice | solution.py:42
  1086.8 184.8 %while.83 = (s32[]{:T(128)}, f32[96,512,16]{1,2,0:T(8,128)S(1)}, f32[512,16]{0,1:T(8,128)S(1)}, f32[16,96,512]{2,1,0:T(8,128)}, f32[16,96,16]{2,1,0:T(8,128)}, /...) while((s32[]{:T(128)}, f32[96,512,16]{1,2,0:T(8,128)S(1)}, ...), condition=%wide.region_23.24_spmd.clone, body=%wide.region_17.23_spmd.clone.sunk | while | flops 15684612 | bytes 12907871 | solution.py:121
  1296.2 50.7 %all-reduce.39 = bf16[1536,160]{0,1:T(8,128)(2,1)} all-reduce(f32[1536,160]{0,1:T(8,128)} %pad_maximum_fusion.5), channel_id=1, replica_groups=mesh['dp'=4,'tensor'=8] {'tensor'}, use_global_device_ids=true, to_apply=%region_24.25 | all-reduce | flops 245760 | bytes 1474560 | tf_op jit(solution)/shard_map/psum | solution.py:277
  1418.0 166.0 %reduce-scatter.21.cloned.1.call-done = f32[192,2048]{1,0:T(8,128)} async-done(((f32[1536,2048]{1,0:T(8,128)}), f32[192,2048]{1,0:T(8,128)}) %reduce-scatter.21.cloned.1.call-update) | async-done | bytes 1572880 | tf_op jit(solution)/shard_map/reduce_scatter | solution.py:302
  1585.9 208.1 %reduce-scatter.19.cloned.1.call-done = f32[192,2048]{1,0:T(8,128)} async-done(((f32[1536,2048]{1,0:T(8,128)}), f32[192,2048]{1,0:T(8,128)}) %reduce-scatter.19.cloned.1.call-update) | async-done | bytes 1572880 | tf_op jit(solution)/shard_map/reduce_scatter | solution.py:241
  1818.9 18.2 reduce-scatter.33.cloned.1.call-done
  1838.5 20.3 reduce-scatter.35.cloned.1.call-done
  1860.2 20.7 %reduce-scatter.31.cloned.1.call-done = f32[32,16]{1,0:T(8,128)} async-done(((f32[128,16]{1,0:T(8,128)}), f32[32,16]{1,0:T(8,128)}) %reduce-scatter.31.cloned.1.call-update) | async-done | bytes 2064
  1882.4 72.6 %reduce-scatter.23.cloned.1.call-done = f32[2,512,512]{1,2,0:T(8,128)} async-done(((f32[2,2048,512]{1,2,0:T(8,128)}), f32[2,512,512]{1,2,0:T(8,128)}) %reduce-scatter.23.cloned.1.call-update) | async-done | bytes 2097168 | tf_op jit(solution)/shard_map/reduce_scatter | solution.py:316
  1968.5 22.1 %psum.23 = f32[512]{0:T(512)} all-reduce(f32[512]{0:T(512)S(1)} %dynamic-slice.1), channel_id=1, replica_groups=mesh['dp'=4,'tensor'=8] {'tensor'}, use_global_device_ids=true, to_apply=%region_29.30 | all-reduce | flops 512 | bytes 4096 | tf_op jit(solution)/shard_map/psum | solution.py:340
  2002.8 47.7 %reduce-scatter.29.cloned.1.call-done = f32[512,512]{1,0:T(8,128)} async-done(((f32[512,2048]{1,0:T(8,128)}), f32[512,512]{1,0:T(8,128)}) %reduce-scatter.29.cloned.1.call-update) | async-done | bytes 1048592 | tf_op jit(solution)/shard_map/reduce_scatter | solution.py:338
  (921 shorter events, 1055.1 us)
Async XLA Ops:
  7.2 81.6 %all-gather.13.cloned.1.call-start = ((), (), s32[]{:S(2)}) async-start(), calls=%async_computation.16 | async-start | bytes 5242880 | tf_op jit(solution)/shard_map/all_gather | solution.py:178
  24.6 24.9 %all-to-all-start.1 = ((bf16[4,48,2048]{2,1,0:T(8,128)(2,1)}), bf16[4,48,2048]{2,1,0:T(8,128)(2,1)S(1)}, u32[]{:S(2)}, u32[]{:S(2)}) async-start(bf16[4,48,2048]{2,1,0:T(8,128)(2,1)} %bitcast.13), calls=%async_computation.1 | async-start | bytes 1572864 | tf_op jit(solution)/shard_map/all_to_all | solution.py:160
  28.1 129.0 %all-gather.11.cloned.1.call-start = ((), (), s32[]{:S(2)}) async-start(), calls=%async_computation.15 | async-start | bytes 7077888 | tf_op jit(solution)/shard_map/all_gather | solution.py:202
  52.7 126.8 %all-gather.15.cloned.1.call-start = ((), (), s32[]{:S(2)}) async-start(), calls=%async_computation.18 | async-start | bytes 2621440 | tf_op jit(solution)/shard_map/all_gather | solution.py:186
  53.4 227.7 %all-gather.17.cloned.1.call-start = ((), (), s32[]{:S(2)}) async-start(), calls=%async_computation.25 | async-start | bytes 7077888 | tf_op jit(solution)/shard_map/all_gather | solution.py:250
  70.8 302.2 %all-reduce.38.cloned.1.call-start = ((), (), s32[]{:S(2)}) async-start(), calls=%async_computation.17 | async-start | bytes 1966080 | tf_op jit(solution)/shard_map/psum | solution.py:224
  76.8 204.3 %copy-start.70 = (f32[1,4,128]{2,1,0:T(4,128)}, f32[1,4,128]{2,1,0:T(4,128)S(1)}, u32[]{:S(2)}) copy-start(f32[1,4,128]{2,1,0:T(4,128)S(1)} %copy.125) | copy-start | bytes 6148
  76.9 204.3 %copy-start.72 = (f32[1,4,128]{2,1,0:T(4,128)}, f32[1,4,128]{2,1,0:T(4,128)S(1)}, u32[]{:S(2)}) copy-start(f32[1,4,128]{2,1,0:T(4,128)S(1)} %copy.126) | copy-start | bytes 6148
  77.0 204.2 %copy-start.76 = (f32[1,4,128]{2,1,0:T(4,128)}, f32[1,4,128]{2,1,0:T(4,128)S(1)}, u32[]{:S(2)}) copy-start(f32[1,4,128]{2,1,0:T(4,128)S(1)} %copy.127) | copy-start | bytes 6148
  88.6 206.2 %copy-start.37 = (bf16[4,128,160]{2,1,0:T(8,128)(2,1)}, bf16[4,128,160]{2,1,0:T(8,128)(2,1)S(1)}, u32[]{:S(2)}) copy-start(bf16[4,128,160]{2,1,0:T(8,128)(2,1)S(1)} %all_gather.42) | copy-start | bytes 491524
  297.6 1286.4 %reduce-scatter.21.cloned.1.call-start = ((), (), s32[]{:S(2)}) async-start(), calls=%async_computation.20 | async-start | bytes 14155776 | tf_op jit(solution)/shard_map/reduce_scatter | solution.py:302
  1378.0 415.9 %reduce-scatter.19.cloned.1.call-start = ((), (), s32[]{:S(2)}) async-start(), calls=%async_computation.19 | async-start | bytes 14155776 | tf_op jit(solution)/shard_map/reduce_scatter | solution.py:241
  1388.3 429.3 %reduce-scatter.37.cloned.1.call-start = ((), (), s32[]{:S(2)}) async-start(), calls=%async_computation.29 | async-start | bytes 81920
  1389.7 447.4 %reduce-scatter.33.cloned.1.call-start = ((), (), s32[]{:S(2)}) async-start(), calls=%async_computation.27 | async-start | bytes 81920
  1390.5 468.3 %reduce-scatter.35.cloned.1.call-start = ((), (), s32[]{:S(2)}) async-start(), calls=%async_computation.28 | async-start | bytes 81920
  1391.3 489.6 %reduce-scatter.31.cloned.1.call-start = ((), (), s32[]{:S(2)}) async-start(), calls=%async_computation.26 | async-start | bytes 81920
  1392.3 562.7 %reduce-scatter.23.cloned.1.call-start = ((), (), s32[]{:S(2)}) async-start(), calls=%async_computation.21 | async-start | bytes 10485760 | tf_op jit(solution)/shard_map/reduce_scatter | solution.py:316
  1405.0 590.3 %reduce-scatter.27.cloned.1.call-start = ((), (), s32[]{:S(2)}) async-start(), calls=%async_computation.23 | async-start | bytes 327680 | tf_op jit(solution)/shard_map/reduce_scatter | solution.py:332
  1407.3 595.5 %reduce-scatter.25.cloned.1.call-start = ((), (), s32[]{:S(2)}) async-start(), calls=%async_computation.22 | async-start | bytes 655360 | tf_op jit(solution)/shard_map/reduce_scatter | solution.py:326
  1410.1 640.4 %reduce-scatter.29.cloned.1.call-start = ((), (), s32[]{:S(2)}) async-start(), calls=%async_computation.24 | async-start | bytes 5242880 | tf_op jit(solution)/shard_map/reduce_scatter | solution.py:338
  1418.0 376.0 %copy-start.24 = (bf16[192,2048]{1,0:T(8,128)(2,1)S(1)}, bf16[192,2048]{1,0:T(8,128)(2,1)}, u32[]{:S(2)}) copy-start(bf16[192,2048]{1,0:T(8,128)(2,1)} %gather_fusion.6) | copy-start | bytes 2359300
  1585.9 210.5 %copy-start.69 = (s32[1024]{0:T(1024)S(1)}, s32[1024]{0:T(1024)}, u32[]{:S(2)}) copy-start(s32[1024]{0:T(1024)} %copy-done.68) | copy-start | bytes 12292
  1798.5 15.5 all-to-all-start.4
  1814.0 179.2 %all-to-all-start.2 = ((bf16[4,48,2048]{2,1,0:T(8,128)(2,1)}), bf16[4,48,2048]{2,1,0:T(8,128)(2,1)S(1)}, u32[]{:S(2)}, u32[]{:S(2)}) async-start(bf16[4,48,2048]{2,1,0:T(8,128)(2,1)} %bitcast.55), calls=%async_computation.3 | async-start | bytes 1572864 | tf_op jit(solution)/shard_map/all_to_all | solution.py:344
  (81 other events, 2301.5 us)
Sparse Core Ops, SparseCore 0:
  9.6 45.6 all-gather.12
  58.0 99.0 all-gather.10
  158.7 20.7 all-gather.14
  182.1 99.0 all-gather.16
  297.7 75.1 all-reduce.37
  1378.2 205.7 reduce-scatter.20
  1587.5 206.3 reduce-scatter.18
  1796.4 18.6 reduce-scatter.36
  1817.6 19.4 reduce-scatter.32
  1839.4 19.3 reduce-scatter.34
  1861.4 19.4 reduce-scatter.30
  1883.3 71.6 reduce-scatter.22
  1958.2 19.9 reduce-scatter.26
  1981.2 21.6 reduce-scatter.24
  2005.9 44.5 reduce-scatter.28
where the time goes:
time: 2090 us; the launch traced here: 2060 us
  waiting for transfers between devices  794 us (38%)
  local copies, waits for them, and re-layouts  506 us (24%)
  other arithmetic  480 us (23%)
  blocking collectives  161 us (8%)
  matrix products  86.1 us (4%)
    reduce_scatter x1, waiting for transfers between devices, shards(): lax.psum_scatter(jnp.dot(piece, out_full, preferred_element_type=jnp.floa...  208 us
    reduce_scatter x1, waiting for transfers between devices, shards(): lax.psum_scatter(jnp.einsum('gkc,kdc->gd', piece, in_full, preferred_elem...  166 us
    all_gather x1, waiting for transfers between devices, shards(): lax.all_gather(dealt_cot, 'tensor', axis=0, tiled=True)  102 us
    reduce_sum x16, other arithmetic, gradient_step(): grad_decay = jnp.sum(through * decay_rate[None], axis=2)  88.3 us
    pad x18, local copies, waits for them, and re-layouts, block_starts(): inclusive = lax.associative_scan(combine, (totals, finals))[1]  86.5 us
    mul x16, other arithmetic, local_back(): return ((decays * adjoint, decays * running), None)  82.2 us
    unnamed x194, local copies, waits for them, and re-layouts  74.1 us
    reduce_scatter x1, waiting for transfers between devices, shards(): lax.psum_scatter(in_weight_grad, 'dp', scatter_dimension=1, tiled=True)  72.6 us
  transfers between devices with their start and end apart: 18, of which 13 were waited for; matrix products, arithmetic and copies ran while one was open for 5% of the time, Pallas kernels for 0%

commit v1 on v0

v1 whole, which is shorter than its diff:
```python
import functools
import jax
import jax.numpy as jnp
from jax import lax
from jax.experimental import pallas as pl
from jax.experimental.pallas import tpu as pltpu

from jax.sharding import PartitionSpec as P

LOG2E = 1.4426950408889634
FAR = 1e30
GROUP_STEP = 16


def softplus(v):
    return jnp.maximum(v, 0.0) + jnp.log1p(jnp.exp(-jnp.abs(v)))


def sigmoid(v):
    return 1.0 / (1.0 + jnp.exp(-v))


def spread_mask(rows, states):
    row = lax.broadcasted_iota(jnp.int32, (rows, GROUP_STEP * states), 0) % GROUP_STEP
    lane = lax.broadcasted_iota(jnp.int32, (rows, GROUP_STEP * states), 1) // states
    return row == lane


def tile_matrix(states, dtype):
    row = lax.broadcasted_iota(jnp.int32, (states, GROUP_STEP * states), 0)
    lane = lax.broadcasted_iota(jnp.int32, (states, GROUP_STEP * states), 1) % states
    return (row == lane).astype(dtype)


def untile_matrix(states, dtype):
    row = lax.broadcasted_iota(jnp.int32, (GROUP_STEP * states, states), 0) % states
    lane = lax.broadcasted_iota(jnp.int32, (GROUP_STEP * states, states), 1)
    return (row == lane).astype(dtype)


NT = (((1,), (1,)), ((), ()))
TN = (((0,), (0,)), ((), ()))


def forward_kernel(low_ref, act_ref, gate_ref, begin_ref, bt_ref, c_ref, dw_ref, bias_ref, rate_ref, skip_ref,
                   pre_ref, y_ref, gated_ref, hist_ref,
                   dtm_s, u_s, h_s):
    states = rate_ref.shape[0]
    chunk = act_ref.shape[0]

    @pl.when(pl.program_id(0) == 0)
    def _():
        h_s[...] = jnp.zeros_like(h_s)

    pre = jnp.dot(low_ref[...], dw_ref[...], preferred_element_type=jnp.float32) + bias_ref[...]
    pre_ref[...] = pre
    dt = softplus(pre)
    act = act_ref[...].astype(jnp.float32)
    u_s[...] = dt * act
    dtm_s[...] = jnp.where(begin_ref[...] > 0.0, FAR, dt)
    rate = rate_ref[...]
    bt = bt_ref[...]
    spread = jnp.where(
        spread_mask(chunk, states),
        jnp.dot(c_ref[...], tile_matrix(states, jnp.bfloat16), preferred_element_type=jnp.float32),
        0.0,
    ).astype(jnp.bfloat16)

    def group(g, h):
        base = pl.multiple_of(g * GROUP_STEP, GROUP_STEP)
        bg = pltpu.roll(bt, (chunk - base) % chunk, 1)
        dtm = dtm_s[pl.ds(base, GROUP_STEP), :]
        u = u_s[pl.ds(base, GROUP_STEP), :]
        for j in range(GROUP_STEP):
            a = jnp.exp2(dtm[j:j + 1, :] * rate)
            h = a * h + u[j:j + 1, :] * bg[:, j:j + 1]
            at = pl.multiple_of((base + j) * states, states)
            hist_ref[pl.ds(at, states), :] = h.astype(jnp.bfloat16)
        return h

    h_s[...] = lax.fori_loop(0, chunk // GROUP_STEP, group, h_s[...])
    width = GROUP_STEP * states
    for g in range(chunk // GROUP_STEP):
        y_ref[g * GROUP_STEP:(g + 1) * GROUP_STEP, :] = jnp.dot(
            spread[g * GROUP_STEP:(g + 1) * GROUP_STEP, :], hist_ref[g * width:(g + 1) * width, :],
            preferred_element_type=jnp.float32)
    y = y_ref[...] + skip_ref[...] * act
    y_ref[...] = y
    gate = gate_ref[...].astype(jnp.float32)
    gated_ref[...] = (y * gate * sigmoid(gate)).astype(jnp.bfloat16)


def scan_forward(low, act, gate, begin, bt, c_values, delta_w, bias, rate, skip, chunk=128):
    tokens, channels = act.shape
    states = rate.shape[0]
    rank = low.shape[1]
    row = lambda i: (i, 0)
    fixed = lambda i: (0, 0)
    return pl.pallas_call(
        forward_kernel,
        name="scan_forward",
        grid=(tokens // chunk,),
        in_specs=[
            pl.BlockSpec((chunk, rank), row),
            pl.BlockSpec((chunk, channels), row),
            pl.BlockSpec((chunk, channels), row),
            pl.BlockSpec((chunk, 1), row),
            pl.BlockSpec((states, chunk), lambda i: (0, i)),
            pl.BlockSpec((chunk, states), row),
            pl.BlockSpec((rank, channels), fixed),
            pl.BlockSpec((1, channels), fixed),
            pl.BlockSpec((states, channels), fixed),
            pl.BlockSpec((1, channels), fixed),
        ],
        out_specs=[
            pl.BlockSpec((chunk, channels), row),
            pl.BlockSpec((chunk, channels), row),
            pl.BlockSpec((chunk, channels), row),
            pl.BlockSpec((chunk * states, channels), row),
        ],
        out_shape=[
            jax.ShapeDtypeStruct((tokens, channels), jnp.float32),
            jax.ShapeDtypeStruct((tokens, channels), jnp.float32),
            jax.ShapeDtypeStruct((tokens, channels), jnp.bfloat16),
            jax.ShapeDtypeStruct((tokens * states, channels), jnp.bfloat16),
        ],
        scratch_shapes=[
            pltpu.VMEM((chunk, channels), jnp.float32),
            pltpu.VMEM((chunk, channels), jnp.float32),
            pltpu.VMEM((states, channels), jnp.float32),
        ],
        compiler_params=pltpu.CompilerParams(dimension_semantics=("arbitrary",), vmem_limit_bytes=48 << 20),
        cost_estimate=pl.CostEstimate(flops=tokens * channels * states * 20, transcendentals=tokens * channels * states, bytes_accessed=tokens * channels * (states * 2 + 20)),
    )(low, act, gate, begin, bt, c_values, delta_w, bias, rate, skip)


def backward_kernel(low_ref, pre_ref, act_ref, gate_ref, gg_ref, y_ref, begin_ref, b_ref, ct_ref,
                    hist_ref, prior_ref, dw_ref, rate_ref, skip_ref,
                    ggate_ref, gact_ref, gpre_ref, glow_ref, gbc_ref, rgrad_ref, dwgrad_ref, rows_ref,
                    dtm_s, u_s, dt_s, gy_s, drive_s, decay_s, carry_s, adj_s, thr_s):
    states = rate_ref.shape[0]
    chunk = act_ref.shape[0]
    step = pl.program_id(0)

    @pl.when(step == 0)
    def _():
        carry_s[...] = jnp.zeros_like(carry_s)
        rgrad_ref[...] = jnp.zeros_like(rgrad_ref)
        dwgrad_ref[...] = jnp.zeros_like(dwgrad_ref)
        rows_ref[...] = jnp.zeros_like(rows_ref)

    pre = pre_ref[...]
    dt = softplus(pre)
    act = act_ref[...].astype(jnp.float32)
    dt_s[...] = dt
    u_s[...] = dt * act
    dtm_s[...] = jnp.where(begin_ref[...] > 0.0, FAR, dt)
    gate = gate_ref[...].astype(jnp.float32)
    sig = sigmoid(gate)
    gg = gg_ref[...].astype(jnp.float32) * sig
    gy = gg * gate
    gy_s[...] = gy
    ggate_ref[...] = (gg * y_ref[...] * (1.0 + gate * (1.0 - sig))).astype(jnp.bfloat16)
    rate = rate_ref[...]
    scale = 1.0 / LOG2E
    ct = ct_ref[...]
    groups = chunk // GROUP_STEP
    width = GROUP_STEP * states

    def one(base, j, carry, rgrad, cg, dtm, dts, gys, prior):
        a = jnp.exp2(dtm[j:j + 1, :] * rate)
        adj = cg[:, j:j + 1] * gys[j:j + 1, :] + carry
        carry = a * adj
        through = carry * prior
        rgrad = rgrad + through * dts[j:j + 1, :]
        at = pl.multiple_of((base + j) * states, states)
        adj_s[pl.ds(at, states), :] = adj.astype(jnp.bfloat16)
        thr_s[pl.ds(at, states), :] = (through * rate).astype(jnp.bfloat16)
        return carry, rgrad

    def group(k, held):
        carry, rgrad = held
        g = groups - 1 - k
        base = pl.multiple_of(g * GROUP_STEP, GROUP_STEP)
        cg = pltpu.roll(ct, (chunk - base) % chunk, 1)
        dtm = dtm_s[pl.ds(base, GROUP_STEP), :]
        dts = dt_s[pl.ds(base, GROUP_STEP), :]
        gys = gy_s[pl.ds(base, GROUP_STEP), :]
        for j in reversed(range(GROUP_STEP)):
            if j > 0:
                at = pl.multiple_of((base + j - 1) * states, states)
                prior = hist_ref[pl.ds(at, states), :].astype(jnp.float32)
            else:
                at = pl.multiple_of(jnp.maximum(base - 1, 0) * states, states)
                prior = jnp.where(base == 0, prior_ref[...].astype(jnp.float32), hist_ref[pl.ds(at, states), :].astype(jnp.float32))
            carry, rgrad = one(base, j, carry, rgrad, cg, dtm, dts, gys, prior)
        return carry, rgrad

    carry, rgrad = lax.fori_loop(0, groups, group, (carry_s[...], rgrad_ref[...]))
    carry_s[...] = carry
    rgrad_ref[...] = rgrad

    mask = spread_mask(GROUP_STEP, states)
    untile = untile_matrix(states, jnp.bfloat16)
    spread_b = jnp.where(
        spread_mask(chunk, states),
        jnp.dot(b_ref[...], tile_matrix(states, jnp.bfloat16), preferred_element_type=jnp.float32),
        0.0,
    ).astype(jnp.bfloat16)
    ones = jnp.where(mask, 1.0, 0.0).astype(jnp.bfloat16)
    ub = u_s[...].astype(jnp.bfloat16)
    gyb = gy.astype(jnp.bfloat16)
    for g in range(groups):
        rows = slice(g * GROUP_STEP, (g + 1) * GROUP_STEP)
        wide = slice(g * width, (g + 1) * width)
        adj = adj_s[wide, :]
        drive_s[rows, :] = jnp.dot(spread_b[rows, :], adj, preferred_element_type=jnp.float32)
        decay_s[rows, :] = jnp.dot(ones, thr_s[wide, :], preferred_element_type=jnp.float32)
        gb = lax.dot_general(ub[rows, :], adj, NT, preferred_element_type=jnp.float32)
        gc = lax.dot_general(gyb[rows, :], hist_ref[wide, :], NT, preferred_element_type=jnp.float32)
        gb = jnp.where(mask, gb, 0.0).astype(jnp.bfloat16)
        gc = jnp.where(mask, gc, 0.0).astype(jnp.bfloat16)
        gbc_ref[rows, :states] = jnp.dot(gb, untile, preferred_element_type=jnp.float32)
        gbc_ref[rows, states:] = jnp.dot(gc, untile, preferred_element_type=jnp.float32)
    drive = drive_s[...]
    gact_ref[...] = drive * dt + gy * skip_ref[...]
    gpre = ((drive * act + decay_s[...] * scale) * sigmoid(pre)).astype(jnp.bfloat16)
    gpre_ref[...] = gpre
    rows_ref[0:1, :] += jnp.sum(gy * act, axis=0, keepdims=True)
    rows_ref[1:2, :] += jnp.sum(gpre.astype(jnp.float32), axis=0, keepdims=True)
    dwgrad_ref[...] += lax.dot_general(low_ref[...], gpre, TN, preferred_element_type=jnp.float32)
    glow_ref[...] = lax.dot_general(gpre, dw_ref[...], NT, preferred_element_type=jnp.float32)


def scan_backward(low, pre, act, gate, gg, y, begin, b_values, ct, hist, delta_w, rate, skip, chunk=128):
    tokens, channels = act.shape
    states = rate.shape[0]
    rank = low.shape[1]
    steps = tokens // chunk
    row = lambda i: (steps - 1 - i, 0)
    fixed = lambda i: (0, 0)
    return pl.pallas_call(
        backward_kernel,
        name="scan_backward",
        grid=(steps,),
        in_specs=[
            pl.BlockSpec((chunk, rank), row),
            pl.BlockSpec((chunk, channels), row),
            pl.BlockSpec((chunk, channels), row),
            pl.BlockSpec((chunk, channels), row),
            pl.BlockSpec((chunk, channels), row),
            pl.BlockSpec((chunk, channels), row),
            pl.BlockSpec((chunk, 1), row),
            pl.BlockSpec((chunk, states), row),
            pl.BlockSpec((states, chunk), lambda i: (0, steps - 1 - i)),
            pl.BlockSpec((chunk * states, channels), row),
            pl.BlockSpec((states, channels), lambda i: (jnp.maximum((steps - 1 - i) * chunk - 1, 0), 0)),
            pl.BlockSpec((rank, channels), fixed),
            pl.BlockSpec((states, channels), fixed),
            pl.BlockSpec((1, channels), fixed),
        ],
        out_specs=[
            pl.BlockSpec((chunk, channels), row),
            pl.BlockSpec((chunk, channels), row),
            pl.BlockSpec((chunk, channels), row),
            pl.BlockSpec((chunk, rank), row),
            pl.BlockSpec((chunk, 2 * states), row),
            pl.BlockSpec((states, channels), fixed),
            pl.BlockSpec((rank, channels), fixed),
            pl.BlockSpec((8, channels), fixed),
        ],
        out_shape=[
            jax.ShapeDtypeStruct((tokens, channels), jnp.bfloat16),
            jax.ShapeDtypeStruct((tokens, channels), jnp.float32),
            jax.ShapeDtypeStruct((tokens, channels), jnp.bfloat16),
            jax.ShapeDtypeStruct((tokens, rank), jnp.float32),
            jax.ShapeDtypeStruct((tokens, 2 * states), jnp.float32),
            jax.ShapeDtypeStruct((states, channels), jnp.float32),
            jax.ShapeDtypeStruct((rank, channels), jnp.float32),
            jax.ShapeDtypeStruct((8, channels), jnp.float32),
        ],
        scratch_shapes=[pltpu.VMEM((chunk, channels), jnp.float32)] * 6
        + [pltpu.VMEM((states, channels), jnp.float32)]
        + [pltpu.VMEM((chunk * states, channels), jnp.bfloat16)] * 2,
        compiler_params=pltpu.CompilerParams(dimension_semantics=("arbitrary",), vmem_limit_bytes=56 << 20),
        cost_estimate=pl.CostEstimate(flops=tokens * channels * states * 40, transcendentals=tokens * channels * states, bytes_accessed=tokens * channels * (states * 2 + 28)),
    )(low, pre, act, gate, gg, y, begin, b_values, ct, hist, hist, delta_w, rate, skip)


EPSILON = 1e-05


def deal_kernel(x_ref, cot_ref, order_ref, gain_ref, me_ref, sendx_ref, sendc_ref, pick_ref, place_ref):
    rows = x_ref.shape[0]
    dp_size = order_ref.shape[0]
    group_tokens = me_ref[1]
    me = me_ref[0]
    pair = rows // dp_size
    order = order_ref[...]
    source = order // group_tokens
    local = order % rows
    before = (
        lax.broadcasted_iota(jnp.int32, (rows, rows), 0) < lax.broadcasted_iota(jnp.int32, (rows, rows), 1)
    ).astype(jnp.bfloat16)
    slots = lax.broadcasted_iota(jnp.int32, (rows, rows), 0)
    chosen = source == me
    rank = jnp.dot(chosen.astype(jnp.bfloat16), before, preferred_element_type=jnp.float32).astype(jnp.int32)
    dest = lax.broadcasted_iota(jnp.int32, (dp_size, rows), 0)
    slot = jnp.where(chosen, dest * pair + rank, -1)
    pick = jnp.zeros((rows, rows), jnp.float32)
    for d in range(dp_size):
        pick += lax.dot_general(
            (slots == slot[d:d + 1, :]).astype(jnp.bfloat16),
            (slots == local[d:d + 1, :]).astype(jnp.bfloat16),
            NT, preferred_element_type=jnp.float32)
    pick = pick.astype(jnp.bfloat16)
    pick_ref[...] = pick
    mine = jnp.sum(jnp.where(dest == me, source, 0), axis=0, keepdims=True)
    held = (mine == dest).astype(jnp.bfloat16)
    ranks = jnp.dot(held, before, preferred_element_type=jnp.float32).astype(jnp.int32)
    arrived = jnp.sum(jnp.where(mine == dest, dest * pair + ranks, 0), axis=0, keepdims=True)
    place_ref[...] = (slots == arrived).astype(jnp.bfloat16)
    x = x_ref[...].astype(jnp.float32)
    rinv = lax.rsqrt(jnp.mean(x * x, axis=1, keepdims=True) + EPSILON)
    normed = (x * rinv * gain_ref[...]).astype(jnp.bfloat16)
    sendx_ref[...] = jnp.dot(pick, normed, preferred_element_type=jnp.float32).astype(jnp.bfloat16)
    sendc_ref[...] = jnp.dot(pick, cot_ref[...], preferred_element_type=jnp.float32).astype(jnp.bfloat16)


def deal(x, cot, order, gain, me):
    rows, width = x.shape
    vm = pl.BlockSpec(memory_space=pltpu.VMEM)
    return pl.pallas_call(
        deal_kernel,
        name="deal",
        in_specs=[vm, vm, vm, vm, pl.BlockSpec(memory_space=pltpu.SMEM)],
        out_specs=[vm] * 4,
        out_shape=[
            jax.ShapeDtypeStruct((rows, width), jnp.bfloat16),
            jax.ShapeDtypeStruct((rows, width), jnp.bfloat16),
            jax.ShapeDtypeStruct((rows, rows), jnp.bfloat16),
            jax.ShapeDtypeStruct((rows, rows), jnp.bfloat16),
        ],
        compiler_params=pltpu.CompilerParams(vmem_limit_bytes=32 << 20),
        cost_estimate=pl.CostEstimate(flops=rows * rows * width * 6, transcendentals=rows, bytes_accessed=rows * width * 8),
    )(x, cot, order, gain, me)


def exact_dot(a, b, dims=(((1,), (0,)), ((), ()))):
    return lax.dot_general(a, b, dims, preferred_element_type=jnp.float32).astype(jnp.bfloat16)


def swap(values, axis):
    return lax.all_to_all(values, axis, split_axis=0, concat_axis=0, tiled=True)


def sum_all(part, axis):
    size = lax.axis_size(axis)
    pieces = part.astype(jnp.bfloat16).reshape((size, -1) + part.shape[1:])
    total = jnp.sum(swap(pieces, axis).astype(jnp.float32), axis=0).astype(jnp.bfloat16)
    everyone = jnp.broadcast_to(total[None], (size,) + total.shape)
    return swap(everyone, axis).reshape(part.shape)


def shifted(values, amount):
    if amount == 0:
        return values
    head = jnp.zeros((amount,) + values.shape[1:], values.dtype)
    return jnp.concatenate([head, values[: values.shape[0] - amount]], axis=0)


def unshifted(values, amount):
    if amount == 0:
        return values
    tail = jnp.zeros((amount,) + values.shape[1:], values.dtype)
    return jnp.concatenate([values[amount:], tail], axis=0)


def shards(
    block_input, norm_gain, in_weight, conv_weight, conv_bias, select_weight, delta_weight, delta_bias,
    decay_log, skip_weight, out_weight, out_cotangent, seq_lengths, deal_order,
):
    rows_dev = block_input.shape[0]
    dp_size = lax.axis_size("dp")
    tensor_size = lax.axis_size("tensor")
    pair = rows_dev // dp_size
    group_tokens = rows_dev * tensor_size
    me = jnp.stack([lax.axis_index("dp"), jnp.int32(group_tokens)]).astype(jnp.int32)
    orders = lax.all_gather(deal_order.reshape(1, rows_dev), "dp", axis=0, tiled=True)
    gain_full = lax.all_gather(norm_gain.reshape(1, -1), "dp", axis=1, tiled=True)
    gain_values = gain_full.astype(jnp.float32)
    send_rows, send_cot, pick, place = deal(block_input, out_cotangent, orders, gain_values, me)
    recv_rows = swap(send_rows.reshape(dp_size, pair, -1), "dp").reshape(rows_dev, -1)
    recv_cot = swap(send_cot.reshape(dp_size, pair, -1), "dp").reshape(rows_dev, -1)
    normed = exact_dot(place, recv_rows, TN)
    dealt_cot = exact_dot(place, recv_cot, TN)
    group_normed = lax.all_gather(normed, "tensor", axis=0, tiled=True)
    group_cot = lax.all_gather(dealt_cot, "tensor", axis=0, tiled=True)
    in_full = lax.all_gather(in_weight, "dp", axis=1, tiled=True)
    out_full = lax.all_gather(out_weight, "dp", axis=1, tiled=True)
    conv_full = lax.all_gather(conv_weight, "dp", axis=2, tiled=True)
    rows_full = lax.all_gather(jnp.stack([conv_bias, delta_bias, skip_weight]), "dp", axis=2, tiled=True)
    select_full = lax.all_gather(select_weight, "dp", axis=1, tiled=True)
    delta_full = lax.all_gather(delta_weight, "dp", axis=0, tiled=True)
    decay_full = lax.all_gather(decay_log.T, "dp", axis=0, tiled=True)
    channels = in_full.shape[2]
    taps = conv_full.shape[0]
    lane_width = rows_full.shape[2]
    states, low_rank = decay_full.shape[0], delta_full.shape[0]
    select_matrix = select_full.reshape(channels, -1)
    conv_taps = conv_full.astype(jnp.float32).reshape(taps, channels)
    conv_shift, delta_shift, skip_values = (
        rows_full[i].astype(jnp.float32).reshape(1, channels) for i in range(3)
    )
    decay_rate = -jnp.exp(decay_full.astype(jnp.float32))
    rate_two = decay_rate * LOG2E
    lengths_row = seq_lengths[0]
    seq_ends = jnp.cumsum(lengths_row)
    begins = seq_ends - lengths_row
    positions = jnp.arange(group_tokens, dtype=jnp.int32)
    inside = (positions[:, None] >= begins[None, :]) & (positions[:, None] < seq_ends[None, :])
    offset = positions - jnp.sum(jnp.where(inside, begins[None, :], 0), axis=1)
    begin = (offset == 0).astype(jnp.float32)[:, None]
    masks = [(offset >= k).astype(jnp.float32)[:, None] for k in range(taps)]
    projected = jnp.einsum("gd,kdc->kgc", group_normed, in_full, preferred_element_type=jnp.float32).astype(jnp.bfloat16)
    inner_in = projected[0].astype(jnp.float32)
    gate = projected[1]
    convolved = conv_shift
    for k in range(taps):
        convolved = convolved + conv_taps[k][None, :] * shifted(inner_in, k) * masks[k]
    activated = jax.nn.silu(convolved).astype(jnp.bfloat16)
    proj = sum_all(jnp.dot(activated, select_matrix, preferred_element_type=jnp.float32), "tensor")
    low = proj[:, :low_rank]
    b_values = proj[:, low_rank:low_rank + states]
    c_values = proj[:, low_rank + states:]
    pre, y, gated, hist = scan_forward(
        low, activated, gate, begin, b_values.T.astype(jnp.float32), c_values, delta_full, delta_shift, rate_two, skip_values)
    mixed = lax.psum_scatter(exact_dot(gated, out_full), "tensor", scatter_dimension=0, tiled=True)
    out_weight_grad = exact_dot(gated, group_cot, TN)
    grad_gated = lax.dot_general(group_cot, out_full, NT, preferred_element_type=jnp.float32)
    grad_gate, grad_act, grad_pre, grad_low, grad_bc, rate_grad, delta_weight_grad, row_grads = scan_backward(
        low, pre, activated, gate, grad_gated, y, begin, b_values, c_values.T.astype(jnp.float32), hist,
        delta_full, rate_two, skip_values)
    decay_grad = rate_grad * decay_rate
    grad_proj = sum_all(jnp.concatenate([grad_low, grad_bc], axis=1), "tensor")
    select_grad = lax.dot_general(activated, grad_proj, TN, preferred_element_type=jnp.float32)
    grad_act = grad_act + lax.dot_general(grad_proj, select_matrix, NT, preferred_element_type=jnp.float32)
    conv_sig = jax.nn.sigmoid(convolved)
    grad_conv = grad_act * conv_sig * (1.0 + convolved * (1.0 - conv_sig))
    conv_bias_grad = jnp.sum(grad_conv, axis=0)
    tap_grads = []
    grad_inner = jnp.zeros_like(grad_conv)
    for k in range(taps):
        masked = grad_conv * masks[k]
        tap_grads.append(jnp.sum(masked * shifted(inner_in, k), axis=0))
        grad_inner = grad_inner + unshifted(masked * conv_taps[k][None, :], k)
    grad_inner = grad_inner.astype(jnp.bfloat16)
    in_grad = jnp.stack([exact_dot(group_normed, grad_inner, TN), exact_dot(group_normed, grad_gate, TN)])
    grad_normed = (
        lax.dot_general(grad_inner, in_full[0], NT, preferred_element_type=jnp.float32)
        + lax.dot_general(grad_gate, in_full[1], NT, preferred_element_type=jnp.float32)
    ).astype(jnp.bfloat16)
    grad_rows = lax.psum_scatter(grad_normed, "tensor", scatter_dimension=0, tiled=True)
    in_weight_grad = lax.psum_scatter(in_grad, "dp", scatter_dimension=1, tiled=True).astype(jnp.float32)
    out_grad = lax.psum_scatter(out_weight_grad, "dp", scatter_dimension=1, tiled=True).astype(jnp.float32)

    def by_lane(values):
        lanes = values.reshape(-1, channels // lane_width, dp_size, lane_width // dp_size)
        return jnp.moveaxis(lanes, 2, 0).reshape(dp_size, -1)

    parts = [
        by_lane(jnp.stack(tap_grads)),
        by_lane(conv_bias_grad),
        by_lane(row_grads[1]),
        by_lane(row_grads[0]),
        decay_grad.reshape(dp_size, -1),
        delta_weight_grad.reshape(dp_size, -1),
        jnp.moveaxis(select_grad.reshape(channels // lane_width, dp_size, -1), 1, 0).reshape(dp_size, -1),
    ]
    sizes = [part.shape[1] for part in parts]
    flat = jnp.concatenate(parts, axis=1)
    fill = -flat.shape[1] % 1024
    flat = jnp.pad(flat, ((0, 0), (0, fill))).astype(jnp.bfloat16).reshape(dp_size, -1, 128)
    flat = jnp.sum(swap(flat, "dp").astype(jnp.float32), axis=0).reshape(-1)
    small, start = [], 0
    for size in sizes:
        small.append(flat[start:start + size])
        start += size
    gain_part = jnp.sum(in_weight.astype(jnp.float32) * in_weight_grad, axis=(0, 2))
    gain_grad = lax.psum(gain_part, "tensor") / norm_gain.astype(jnp.float32)
    home_out = swap(exact_dot(place, mixed).reshape(dp_size, pair, -1), "dp").reshape(rows_dev, -1)
    home_grad = swap(exact_dot(place, grad_rows).reshape(dp_size, pair, -1), "dp").reshape(rows_dev, -1)
    rows_float = block_input.astype(jnp.float32)
    block_output = (rows_float + lax.dot_general(pick, home_out, TN, preferred_element_type=jnp.float32)).astype(jnp.bfloat16)
    inverse_rms = lax.rsqrt(jnp.mean(rows_float * rows_float, axis=1, keepdims=True) + EPSILON)
    unit_rows = rows_float * inverse_rms
    scaled = lax.dot_general(pick, home_grad, TN, preferred_element_type=jnp.float32) * gain_values
    input_grad = (
        out_cotangent.astype(jnp.float32)
        + inverse_rms * (scaled - unit_rows * jnp.mean(scaled * unit_rows, axis=1, keepdims=True))
    ).astype(jnp.bfloat16)
    return (
        block_output,
        input_grad,
        gain_grad,
        in_weight_grad,
        small[0].reshape(conv_weight.shape),
        small[1].reshape(conv_bias.shape),
        small[6].reshape(select_weight.shape),
        small[5].reshape(delta_weight.shape),
        small[2].reshape(delta_bias.shape),
        small[4].reshape(decay_log.shape[1], decay_log.shape[0]).T,
        small[3].reshape(skip_weight.shape),
        out_grad,
    )


def solution(mesh):
    return jax.shard_map(
        shards,
        mesh=mesh,
        in_specs=(
            P(("dp", "tensor"), None),
            P("dp"),
            P(None, "dp", "tensor"),
            P(None, "tensor", "dp"),
            P("tensor", "dp"),
            P("tensor", "dp", None),
            P("dp", "tensor"),
            P("tensor", "dp"),
            P("tensor", "dp"),
            P("tensor", "dp"),
            P("tensor", "dp"),
            P(("dp", "tensor"), None),
            P("dp", None),
            P(("dp", "tensor")),
        ),
        out_specs=(
            P(("dp", "tensor"), None),
            P(("dp", "tensor"), None),
            P("dp"),
            P(None, "dp", "tensor"),
            P(None, "tensor", "dp"),
            P("tensor", "dp"),
            P("tensor", "dp", None),
            P("dp", "tensor"),
            P("tensor", "dp"),
            P("tensor", "dp"),
            P("tensor", "dp"),
            P("tensor", "dp"),
        ),
        check_vma=False,
    )
```

time: 2090 us -> 686 us (0.33); the launches traced: 2060 us -> 677 us
  waiting for transfers between devices: 794 us -> 217 us
  local copies, waits for them, and re-layouts: 506 us -> 40.2 us
  other arithmetic: 480 us -> 26.3 us
  Pallas kernels: 0 us -> 110 us
    reduce_scatter x5 -> x3, waiting for transfers between devices: 454 us -> 112 us  [the longest x1 72.1 us: shards(): lax.psum_scatter(grad_normed, 'tensor', scatter_dimension=0, tiled=True)]
    mul x110 -> x4, other arithmetic: 231 us -> 1.27 us  [the longest x3 1.26 us: shards(): grad_inner = grad_inner + unshifted(masked * conv_taps[k][None, :], k)]
    mul x272 -> x0, local copies, waits for them, and re-layouts: 158 us -> none  [the longest x64 60.4 us: step_terms(): delta_step[:, :, None] * decay_rate[None]]
    reduce_sum x34 -> x4, other arithmetic: 123 us -> 3.09 us  [the longest x1 2.82 us: shards(): jnp.sum(in_weight.astype(jnp.float32) * in_weight_grad, axis=(0, 2))]
    pallas_call x0 -> x3, Pallas kernels: none -> 110 us  [the longest x1 76.2 us: scan_backward(): pl.pallas_call(backward_kernel, name='scan_backward', grid=(steps,), in_s...]
    all_gather x3, waiting for transfers between devices: 108 us -> 8.25 us  [the longest x1 8.23 us: shards(): group_cot = lax.all_gather(dealt_cot, 'tensor', axis=0, tiled=True)]
    pad x18 -> x0, local copies, waits for them, and re-layouts: 86.5 us -> none  [block_starts(): inclusive = lax.associative_scan(combine, (totals, finals))[1]]
    all_to_all x2 -> x4, blocking collectives: 21.8 us -> 107 us  [swap(): return lax.all_to_all(values, axis, split_axis=0, concat_axis=0, tiled=True)]
  transfers between devices with their start and end apart: 18 -> 13, of which waited for: 13 -> 7; matrix products, arithmetic and copies ran while one was open for 5% -> 20% of each run, Pallas kernels for 0% -> 16%
where the time goes in v1:
time: 686 us; the launch traced here: 677 us
  waiting for transfers between devices  217 us (32%)
  blocking collectives  167 us (24%)
  Pallas kernels  110 us (16%)
  matrix products  80.8 us (12%)
  local copies, waits for them, and re-layouts  40.2 us (6%)
  other arithmetic  26.3 us (4%)
  starting transfers between devices  19.6 us (3%)
  between operations  16.1 us (2%)
    all_to_all x4, blocking collectives, swap(): return lax.all_to_all(values, axis, split_axis=0, concat_axis=0, tiled=True)  107 us
    pallas_call x1, Pallas kernels, scan_backward(): pl.pallas_call(backward_kernel, name='scan_backward', grid=(steps,), in_s...  76.2 us
    reduce_scatter x1, waiting for transfers between devices, shards(): lax.psum_scatter(grad_normed, 'tensor', scatter_dimension=0, tiled=True)  72.1 us
    all_gather x1, waiting for transfers between devices, shards(): group_normed = lax.all_gather(normed, 'tensor', axis=0, tiled=True)  71.4 us
    reduce_scatter x1, waiting for transfers between devices, shards(): lax.psum_scatter(in_grad, 'dp', scatter_dimension=1, tiled=True)  39.7 us
    dot_general x8, matrix products, exact_dot(): lax.dot_general(a, b, dims, preferred_element_type=jnp.float32)  36.4 us
    pallas_call x1, Pallas kernels, scan_forward(): pl.pallas_call(forward_kernel, name='scan_forward', grid=(tokens // chunk...  31.7 us
    all_to_all x5, waiting for transfers between devices, swap(): return lax.all_to_all(values, axis, split_axis=0, concat_axis=0, tiled=True)  23.6 us
  transfers between devices with their start and end apart: 13, of which 7 were waited for; matrix products, arithmetic and copies ran while one was open for 20% of the time, Pallas kernels for 16%

profile of v1, /device:TPU:0, one launch (start us, length us, event | category | flops | bytes accessed | tf_op | source)
XLA Modules:
  0.0 676.6 jit_solution(345402891671438196)
XLA Ops:
  11.4 6.4 all-reduce.7
  27.2 22.8 %all_to_all.45 = bf16[4,48,2048]{2,1,0:T(8,128)(2,1)S(1)} all-to-all(bf16[4,48,2048]{2,1,0:T(8,128)(2,1)S(1)} %bitcast.149), channel_id=1, replica_groups=mesh['dp'=4,'tensor'=8] {'dp'}, dimensions={0} | all-to-all | bytes 1572864 | tf_op jit(solution)/shard_map/all_to_all | solution.py:354
  52.1 14.1 %all_to_all.46 = bf16[4,48,2048]{2,1,0:T(8,128)(2,1)S(1)} all-to-all(bf16[4,48,2048]{2,1,0:T(8,128)(2,1)S(1)} %bitcast.148), channel_id=1, replica_groups=mesh['dp'=4,'tensor'=8] {'dp'}, dimensions={0} | all-to-all | bytes 1572864 | tf_op jit(solution)/shard_map/all_to_all | solution.py:354
  79.5 5.9 all_gather.39
  85.6 71.4 %all-gather.9.cloned.1.call-done = bf16[1536,2048]{1,0:T(8,128)(2,1)} async-done(((bf16[192,2048]{1,0:T(8,128)(2,1)}), bf16[1536,2048]{1,0:T(8,128)(2,1)}) %all-gather.9.cloned.1.call-update) | async-done | bytes 6291472 | tf_op jit(solution)/shard_map/all_gather | solution.py:397
  157.1 10.0 %fusion.7 = bf16[2,1536,512]{2,1,0:T(8,128)(2,1)S(1)} fusion(bf16[2,2048,512]{2,1,0:T(8,128)(2,1)} %all-gather.11.cloned.1.call-done, bf16[1536,2048]{1,0:T(8,128)(2,1)} %all-gather.9.cloned.1.call-done), kind=kOutput, calls=%fused_computation.9 | convolution fusion | flops 6444023808 | bytes 13631488 | tf_op jit(solution)/shard_map/gd,kdc->kgc/dot_general | solution.py:425
  178.2 31.6 %all_to_all.47 = bf16[8,192,160]{1,2,0:T(8,128)(2,1)S(1)} all-to-all(bf16[8,192,160]{1,2,0:T(8,128)(2,1)S(1)} %copy.121), channel_id=1, replica_groups=mesh['dp'=4,'tensor'=8] {'tensor'}, dimensions={0} | all-to-all | bytes 983040 | tf_op jit(solution)/shard_map/all_to_all | solution.py:354
  227.4 10.1 %all-to-all-done.2 = bf16[8,192,160]{1,2,0:T(8,128)(2,1)S(1)} async-done(((bf16[8,192,160]{1,2,0:T(8,128)(2,1)}), bf16[8,192,160]{1,2,0:T(8,128)(2,1)S(1)}, u32[]{:S(2)}, u32[]{:S(2)}) %all-to-all-start.2) | async-done | bytes 491552 | tf_op jit(solution)/shard_map/all_to_all | solution.py:354
  247.0 31.7 %scan_forward.1 = (f32[1536,512]{1,0:T(8,128)}, f32[1536,512]{1,0:T(8,128)}, bf16[1536,512]{1,0:T(8,128)(2,1)S(1)}, bf16[24576,512]{1,0:T(8,128)(2,1)}) custom-call(bf16[1536,128]{1,0:T(8,128)(2,1)S(1)} %copy.127.low_ref, bf16[1536,512]{1,0:T(8,128)(2,1)S(1)} %get-tuple-element.57.act_ref, bf16[1536,512]{1,0:T(8,128)(2,1)} %get-tuple-element.64.gate_ref, ...), custom_call_target="tpu_custom_call" | custom-call | flops 251658240 | bytes 40894464 | tf_op jit(solution)/shard_map/scan_forward/pallas_call | solution.py:99
  279.8 8.2 %convolution_convert_fusion = bf16[1536,2048]{1,0:T(8,128)(2,1)} fusion(bf16[1536,512]{1,0:T(8,128)(2,1)} %copy-done.12, bf16[512,2048]{1,0:T(8,128)(2,1)} %all-gather.13.cloned.1.call-done), kind=kOutput, calls=%fused_computation.1 | convolution fusion | flops 3224371200 | bytes 9961472 | tf_op jit(solution)/shard_map/dot_general | solution.py:350
  288.1 8.2 %all-gather.15.cloned.1.call-done = bf16[1536,2048]{1,0:T(8,128)(2,1)} async-done(((bf16[192,2048]{1,0:T(8,128)(2,1)}), bf16[1536,2048]{1,0:T(8,128)(2,1)}) %all-gather.15.cloned.1.call-update) | async-done | bytes 6291472 | tf_op jit(solution)/shard_map/all_gather | solution.py:398
  296.3 8.0 %fusion.34.gg_ref = f32[1536,512]{1,0:T(8,128)} fusion(bf16[1536,2048]{1,0:T(8,128)(2,1)} %all-gather.15.cloned.1.call-done, bf16[512,2048]{1,0:T(8,128)(2,1)S(1)} %copy-done.56), kind=kOutput, calls=%fused_computation.108 | convolution fusion | flops 3221225472 | bytes 11534336 | tf_op jit(solution)/shard_map/dot_general | solution.py:440
  305.2 76.2 %scan_backward.1 = (bf16[1536,512]{1,0:T(8,128)(2,1)}, f32[1536,512]{1,0:T(8,128)}, bf16[1536,512]{1,0:T(8,128)(2,1)}, f32[1536,128]{1,0:T(8,128)}, f32[1536,32]...) custom-call(bf16[1536,128]{1,0:T(8,128)(2,1)} %copy-done.5, ...), custom_call_target="tpu_custom_call" | custom-call | flops 503316480 | bytes 47185920 | tf_op jit(solution)/shard_map/scan_backward/pallas_call | solution.py:242
  384.3 38.4 %all_to_all.48 = bf16[8,192,160]{1,2,0:T(8,128)(2,1)S(1)} all-to-all(bf16[8,192,160]{1,2,0:T(8,128)(2,1)S(1)} %pad_maximum_fusion.1), channel_id=1, replica_groups=mesh['dp'=4,'tensor'=8] {'tensor'}, dimensions={0} | all-to-all | bytes 983040 | tf_op jit(solution)/shard_map/all_to_all | solution.py:354
  427.9 7.5 %convolution_convert_fusion.1 = bf16[512,2048]{1,0:T(8,128)(2,1)} fusion(bf16[1536,512]{1,0:T(8,128)(2,1)S(1)} %copy-done.13, bf16[1536,2048]{1,0:T(8,128)(2,1)} %all-gather.15.cloned.1.call-done), kind=kOutput, calls=%fused_computation.30 | convolution fusion | flops 3222274048 | bytes 9961472 | tf_op jit(solution)/shard_map/dot_general | solution.py:350
  435.5 9.3 %all-to-all-done.6 = bf16[8,192,160]{1,2,0:T(8,128)(2,1)} async-done(((bf16[8,192,160]{1,2,0:T(8,128)(2,1)}), bf16[8,192,160]{1,2,0:T(8,128)(2,1)}, u32[]{:S(2)}, u32[]{:S(2)}) %all-to-all-start.6) | async-done | bytes 491552 | tf_op jit(solution)/shard_map/all_to_all | solution.py:354
  449.6 7.8 %multiply_reduce_fusion.2 = (bf16[512]{0:T(512)(128)(2,1)}, f32[1536,512]{1,0:T(8,128)S(1)}, bf16[512]{0:T(512)(128)(2,1)S(1)}, f32[1536,512]{1,0:T(8,128)S(1)},...) fusion(f32[1535,512]{1,0:T(8,128)} %copy-done.16, f32[1536]{0:T(1024)S(1)} %copy-done.31, ...), kind=kOutput, calls=%fused_computation.26 | convolution fusion | flops 265812480 | bytes 28976128 | tf_op jit(solution)/shard_map/dot_general | solution.py:447
  463.2 6.4 fusion.19
  469.6 8.2 %add_convert_fusion = bf16[1536,2048]{1,0:T(8,128)(2,1)} fusion(f32[1536,2048]{1,0:T(8,128)} %fusion.19, bf16[1536,512]{1,0:T(8,128)(2,1)S(1)} %copy-done.57, bf16[2,2048,512]{2,1,0:T(8,128)(2,1)S(1)} %copy-done.55), kind=kOutput, calls=%fused_computation | convolution fusion | flops 3227516928 | bytes 22544384 | tf_op jit(solution)/shard_map/dot_general | solution.py:461
  478.1 6.7 fusion.17
  484.8 6.7 fusion.16
  521.6 72.1 %reduce-scatter.7.cloned.1.call-done = bf16[192,2048]{1,0:T(8,128)(2,1)} async-done(((bf16[1536,2048]{1,0:T(8,128)(2,1)}), bf16[192,2048]{1,0:T(8,128)(2,1)}) %reduce-scatter.7.cloned.1.call-update) | async-done | bytes 786448 | tf_op jit(solution)/shard_map/reduce_scatter | solution.py:463
  600.5 39.7 %reduce-scatter.9.cloned.1.call-done = bf16[2,512,512]{2,1,0:T(8,128)(2,1)} async-done(((bf16[2,2048,512]{2,1,0:T(8,128)(2,1)}), bf16[2,512,512]{2,1,0:T(8,128)(2,1)}) %reduce-scatter.9.cloned.1.call-update) | async-done | bytes 1048592 | tf_op jit(solution)/shard_map/reduce_scatter | solution.py:464
  643.0 21.5 %psum.7 = f32[512]{0:T(512)S(1)} all-reduce(f32[512]{0:T(512)S(1)} %get-tuple-element.55), channel_id=1, replica_groups=mesh['dp'=4,'tensor'=8] {'tensor'}, use_global_device_ids=true, to_apply=%region_10.11 | all-reduce | flops 512 | bytes 4096 | tf_op jit(solution)/shard_map/psum | solution.py:490
  (275 shorter events, 131.8 us)
Async XLA Ops:
  7.2 78.4 %all-gather.11.cloned.1.call-start = ((), (), s32[]{:S(2)}) async-start(), calls=%async_computation.14 | async-start | bytes 5242880 | tf_op jit(solution)/shard_map/all_gather | solution.py:399
  7.9 149.2 %all-gather.9.cloned.1.call-start = ((), (), s32[]{:S(2)}) async-start(), calls=%async_computation.13 | async-start | bytes 7077888 | tf_op jit(solution)/shard_map/all_gather | solution.py:397
  51.4 228.5 %all-gather.13.cloned.1.call-start = ((), (), s32[]{:S(2)}) async-start(), calls=%async_computation.15 | async-start | bytes 2621440 | tf_op jit(solution)/shard_map/all_gather | solution.py:400
  52.1 244.2 %all-gather.15.cloned.1.call-start = ((), (), s32[]{:S(2)}) async-start(), calls=%async_computation.17 | async-start | bytes 7077888 | tf_op jit(solution)/shard_map/all_gather | solution.py:398
  79.3 90.8 %copy-start.39 = (f32[1,4,128]{2,1,0:T(4,128)}, f32[1,4,128]{2,1,0:T(4,128)S(1)}, u32[]{:S(2)}) copy-start(f32[1,4,128]{2,1,0:T(4,128)S(1)} %copy.117) | copy-start | bytes 6148
  79.4 90.7 %copy-start.43 = (f32[1,4,128]{2,1,0:T(4,128)}, f32[1,4,128]{2,1,0:T(4,128)S(1)}, u32[]{:S(2)}) copy-start(f32[1,4,128]{2,1,0:T(4,128)S(1)} %copy.118) | copy-start | bytes 6148
  79.5 90.7 %copy-start.41 = (f32[1,4,128]{2,1,0:T(4,128)}, f32[1,4,128]{2,1,0:T(4,128)S(1)}, u32[]{:S(2)}) copy-start(f32[1,4,128]{2,1,0:T(4,128)S(1)} %copy.119) | copy-start | bytes 6148
  79.5 90.6 %copy-start.45 = (f32[1,4,128]{2,1,0:T(4,128)}, f32[1,4,128]{2,1,0:T(4,128)S(1)}, u32[]{:S(2)}) copy-start(f32[1,4,128]{2,1,0:T(4,128)S(1)} %copy.120) | copy-start | bytes 6148
  85.4 91.4 %copy-start.22 = (bf16[4,128,160]{2,1,0:T(8,128)(2,1)}, bf16[4,128,160]{2,1,0:T(8,128)(2,1)S(1)}, u32[]{:S(2)}) copy-start(bf16[4,128,160]{2,1,0:T(8,128)(2,1)S(1)} %all_gather.39) | copy-start | bytes 491524
  85.5 81.6 %copy-start.28 = (s32[1536]{0:T(1024)}, s32[1536]{0:T(1024)S(1)}, u32[]{:S(2)}) copy-start(s32[1536]{0:T(1024)S(1)} %select_reduce_fusion) | copy-start | bytes 18436
  85.6 84.6 %copy-start.26 = (f32[1536]{0:T(1024)}, f32[1536]{0:T(1024)S(1)}, u32[]{:S(2)}) copy-start(f32[1536]{0:T(1024)S(1)} %get-tuple-element.77) | copy-start | bytes 18436
  85.6 84.6 %copy-start.30 = (f32[1536]{0:T(1024)}, f32[1536]{0:T(1024)S(1)}, u32[]{:S(2)}) copy-start(f32[1536]{0:T(1024)S(1)} %get-tuple-element.78) | copy-start | bytes 18436
  85.6 84.6 %copy-start.32 = (f32[1536]{0:T(1024)}, f32[1536]{0:T(1024)S(1)}, u32[]{:S(2)}) copy-start(f32[1536]{0:T(1024)S(1)} %get-tuple-element.79) | copy-start | bytes 18436
  85.6 84.6 %copy-start.34 = (f32[1536]{0:T(1024)}, f32[1536]{0:T(1024)S(1)}, u32[]{:S(2)}) copy-start(f32[1536]{0:T(1024)S(1)} %get-tuple-element.80) | copy-start | bytes 18436
  210.8 26.8 %all-to-all-start.2 = ((bf16[8,192,160]{1,2,0:T(8,128)(2,1)}), bf16[8,192,160]{1,2,0:T(8,128)(2,1)S(1)}, u32[]{:S(2)}, u32[]{:S(2)}) async-start(bf16[8,192,160]{1,2,0:T(8,128)(2,1)} %broadcast_in_dim.15), calls=%async_computation.2 | async-start | bytes 1310720 | tf_op jit(solution)/shard_map/all_to_all | solution.py:354
  214.3 290.2 %reduce-scatter.5.cloned.1.call-start = ((), (), s32[]{:S(2)}) async-start(), calls=%async_computation.16 | async-start | bytes 7077888 | tf_op jit(solution)/shard_map/reduce_scatter | solution.py:438
  423.7 21.2 %all-to-all-start.6 = ((bf16[8,192,160]{1,2,0:T(8,128)(2,1)}), bf16[8,192,160]{1,2,0:T(8,128)(2,1)}, u32[]{:S(2)}, u32[]{:S(2)}) async-start(bf16[8,192,160]{1,2,0:T(8,128)(2,1)} %broadcast_in_dim.16), calls=%async_computation.7 | async-start | bytes 1310720 | tf_op jit(solution)/shard_map/all_to_all | solution.py:354
  427.9 91.6 %reduce-scatter.11.cloned.1.call-start = ((), (), s32[]{:S(2)}) async-start(), calls=%async_computation.20 | async-start | bytes 2621440 | tf_op jit(solution)/shard_map/reduce_scatter | solution.py:465
  435.5 158.2 %reduce-scatter.7.cloned.1.call-start = ((), (), s32[]{:S(2)}) async-start(), calls=%async_computation.18 | async-start | bytes 7077888 | tf_op jit(solution)/shard_map/reduce_scatter | solution.py:463
  477.8 162.3 %reduce-scatter.9.cloned.1.call-start = ((), (), s32[]{:S(2)}) async-start(), calls=%async_computation.19 | async-start | bytes 5242880 | tf_op jit(solution)/shard_map/reduce_scatter | solution.py:464
  501.1 10.1 %all-to-all-start.8 = ((bf16[4,312,128]{2,1,0:T(8,128)(2,1)}), bf16[4,312,128]{2,1,0:T(8,128)(2,1)S(1)}, u32[]{:S(2)}, u32[]{:S(2)}) async-start(bf16[4,312,128]{2,1,0:T(8,128)(2,1)} %bitcast.143), calls=%async_computation.11 | async-start | bytes 638976 | tf_op jit(solution)/shard_map/all_to_all | solution.py:354
  511.2 85.0 %all-to-all-start.3 = ((bf16[4,48,2048]{2,1,0:T(8,128)(2,1)}), bf16[4,48,2048]{2,1,0:T(8,128)(2,1)S(1)}, u32[]{:S(2)}, u32[]{:S(2)}) async-start(bf16[4,48,2048]{2,1,0:T(8,128)(2,1)} %bitcast.30), calls=%async_computation.4 | async-start | bytes 1572864 | tf_op jit(solution)/shard_map/all_to_all | solution.py:354
  514.7 125.5 %copy-start.21 = (bf16[2,512,512]{2,1,0:T(8,128)(2,1)S(1)}, bf16[2,512,512]{2,1,0:T(8,128)(2,1)}, u32[]{:S(2)}) copy-start(bf16[2,512,512]{2,1,0:T(8,128)(2,1)} %param.16) | copy-start | bytes 3145732
  596.1 70.2 %all-to-all-start.7 = ((bf16[4,48,2048]{2,1,0:T(8,128)(2,1)}), bf16[4,48,2048]{2,1,0:T(8,128)(2,1)}, u32[]{:S(2)}, u32[]{:S(2)}) async-start(bf16[4,48,2048]{2,1,0:T(8,128)(2,1)} %bitcast.39), calls=%async_computation.9 | async-start | bytes 1572864 | tf_op jit(solution)/shard_map/all_to_all | solution.py:354
  (48 other events, 821.4 us)
Sparse Core Ops, SparseCore 0:
  9.6 45.5 all-gather.10
  58.0 99.0 all-gather.8
  158.6 20.7 all-gather.12
  182.1 114.2 all-gather.14
  299.7 130.2 reduce-scatter.4
  435.6 32.5 reduce-scatter.10
  478.0 115.7 reduce-scatter.6
  596.4 43.6 reduce-scatter.8
